TPU v7x, 128 devices: a whole 4x4x4 slice. The times are simulated.
128 devices in a mesh: row: 16 (over y, z), col: 8 (over x, core).
Axes of the slice: x: 4, y: 4, z: 4, core: 2. Of those that a mesh axis runs over, the one named last changes fastest.
Arguments:
- blocks: bfloat16 [16, 8, 128, 4096], P('row', 'col'), may hold values from -0.25 to 0.25
- block_row: int32 [16, 8, 128], P('row', 'col'), may hold values from 0 to 15
- block_col: int32 [16, 8, 128], P('row', 'col'), may hold values from 0 to 31
- counts: int32 [16, 8], P('row', 'col'), may hold values from 0 to 128, as said below
- vectors: float32 [256, 4096], P(('col', 'row')), may hold values from -6 to 6
- row_mass: float32 [256, 64], P(('row', 'col')), may hold values from 0.25 to 4
- col_mass: float32 [256, 64], P(('col', 'row')), may hold values from 0.25 to 4
Outputs:
- subspace: float32 [256, 4096], P(('col', 'row'))
Inputs may be any that keep to these rules, and one draw needn't show every extreme that they name: `counts`: in every row panel one tile uses all 128 slots; every other tile uses at most 8.
All inputs are finite; a program needn't handle non-finite values.
Results may differ from a plain program's by a relative error of at most 0.0085.
Values may be sent and summed in bfloat16 or wider, within the bound.
A program may use at most 64 MiB of HBM per device.

v0:
```python
import jax
import jax.numpy as jnp
from jax import lax
from jax.sharding import PartitionSpec as P

ITERS = 4


def rotate(projected, gram):
    lower = jnp.linalg.cholesky(gram)
    inverse = lax.linalg.triangular_solve(
        lower, jnp.eye(gram.shape[0], dtype=jnp.float32), left_side=True, lower=True
    )
    return jnp.einsum(
        "kl,bli->bki",
        inverse,
        projected,
        precision=lax.Precision.HIGHEST,
        preferred_element_type=jnp.float32,
    )


def local_gram(projected):
    return jnp.einsum(
        "bki,bli->kl",
        projected,
        projected,
        precision=lax.Precision.HIGHEST,
        preferred_element_type=jnp.float32,
    )


def per_device(blocks, block_row, block_col, counts, vectors, row_mass, col_mass):
    tile = blocks[0, 0]
    n_cap = tile.shape[0]
    bsize = row_mass.shape[1]
    vecs = vectors.shape[1] // bsize
    own = vectors.shape[0]
    n_row = lax.axis_size("row")
    n_col = lax.axis_size("col")
    row_panel = own * n_col
    col_panel = own * n_row
    total_boxes = float(own * bsize * n_row * n_col)
    rows_idx = block_row[0, 0]
    cols_idx = block_col[0, 0]
    live = jnp.arange(n_cap) < counts[0, 0]
    fwd_ids = jnp.where(live, rows_idx, row_panel)
    bwd_ids = jnp.where(live, cols_idx, col_panel)
    square = tile.reshape(n_cap, bsize, bsize)
    col_mass_panel = lax.all_gather(col_mass, "row", axis=0, tiled=True)
    row_mass_panel = lax.all_gather(row_mass, "col", axis=0, tiled=True)
    inv_col = 1.0 / jnp.sqrt(col_mass_panel)
    current = lax.all_gather(vectors, "row", axis=0, tiled=True).reshape(col_panel, vecs, bsize)
    for step in range(ITERS):
        scaled = (current * inv_col[:, None, :]).astype(jnp.bfloat16)
        forward_taken = jnp.take(scaled, cols_idx, axis=0)
        forward_product = jnp.einsum(
            "bij,bkj->bki", square, forward_taken, preferred_element_type=jnp.float32
        )
        forward_summed = jax.ops.segment_sum(forward_product, fwd_ids, num_segments=row_panel + 1)
        rows_sum = lax.psum(forward_summed[:row_panel], "col")
        weighted = (rows_sum * row_mass_panel[:, None, :]).astype(jnp.bfloat16)
        taken = jnp.take(weighted, rows_idx, axis=0)
        product = jnp.einsum("bij,bki->bkj", square, taken, preferred_element_type=jnp.float32)
        summed = jax.ops.segment_sum(product, bwd_ids, num_segments=col_panel + 1)
        cols_sum = lax.psum(summed[:col_panel], "row")
        projected = cols_sum * inv_col[:, None, :]
        gram = lax.psum(local_gram(projected), "col") / total_boxes
        current = rotate(projected, gram)
    me = lax.axis_index("row")
    mine = lax.dynamic_slice_in_dim(current, me * own, own, 0)
    return mine.reshape(own, vecs * bsize)


def solution(mesh):
    in_specs = (
        P("row", "col", None, None),
        P("row", "col", None),
        P("row", "col", None),
        P("row", "col"),
        P(("col", "row"), None),
        P(("row", "col"), None),
        P(("col", "row"), None),
    )
    out_specs = P(("col", "row"), None)
    return jax.shard_map(
        per_device, mesh=mesh, in_specs=in_specs, out_specs=out_specs, check_vma=False
    )
```

profile of v0, /device:TPU:0, one launch (start us, length us, event | category | flops | bytes accessed | tf_op | source)
XLA Modules:
  0.0 997.5 jit_solution(7439342869983005372)
XLA Ops:
  7.9 24.9 %all-gather.1 = f32[16,2,64]{2,1,0:T(2,128)S(1)} all-gather(f32[1,2,64]{2,1,0:T(2,128)} %bitcast.111), channel_id=1, replica_groups=mesh['row'=16,'col'=8] {'row'}, dimensions={0}, use_global_device_ids=true | all-gather | bytes 8704 | tf_op jit(solution)/shard_map/all_gather | solution.py:50
  32.8 23.5 %all-gather = f32[16,2,4096]{2,1,0:T(2,128)S(1)} all-gather(f32[1,2,4096]{2,1,0:T(2,128)} %bitcast.110), channel_id=1, replica_groups=mesh['row'=16,'col'=8] {'row'}, dimensions={0}, use_global_device_ids=true | all-gather | bytes 557056 | tf_op jit(solution)/shard_map/all_gather | solution.py:53
  70.6 13.5 %scatter_fusion = f32[17,64,64]{2,1,0:T(8,128)S(1)} fusion(f32[17,64,64]{2,1,0:T(8,128)S(1)} %broadcast.82.clone.2, s32[128]{0:T(128)S(1)} %get-tuple-element.8, f32[128,64,64]{2,1,0:T(8,128)} %fusion.14), kind=kCustom, calls=%fused_computation.8 | custom fusion | flops 524288 | bytes 6291968 | tf_op jit(solution)/shard_map/scatter-add | solution.py:60
  85.1 10.7 %all-gather.2 = f32[8,2,64]{2,1,0:T(2,128)S(1)} all-gather(f32[1,2,64]{2,1,0:T(2,128)S(1)} %bitcast.112), channel_id=1, replica_groups=mesh['row'=16,'col'=8] {'col'}, dimensions={0}, use_global_device_ids=true | all-gather | bytes 4608 | tf_op jit(solution)/shard_map/all_gather | solution.py:51
  95.8 48.5 %all-reduce.9.cloned.1.call-done = f32[16,64,64]{2,1,0:T(8,128)} async-done(((f32[16,64,64]{2,1,0:T(8,128)}), f32[16,64,64]{2,1,0:T(8,128)}) %all-reduce.9.cloned.1.call-update) | async-done | bytes 262160 | tf_op jit(solution)/shard_map/psum | solution.py:61
  152.0 13.5 %scatter_fusion.1 = f32[33,64,64]{2,1,0:T(8,128)S(1)} fusion(f32[33,64,64]{2,1,0:T(8,128)S(1)} %broadcast.81.clone.2, s32[128]{0:T(128)S(1)} %get-tuple-element.6, f32[128,64,64]{2,1,0:T(8,128)} %fusion.12), kind=kCustom, calls=%fused_computation.9 | custom fusion | flops 524288 | bytes 6291968 | tf_op jit(solution)/shard_map/scatter-add | solution.py:65
  166.7 86.6 %all-reduce.11.cloned.1.call-done = f32[32,64,64]{2,1,0:T(8,128)} async-done(((f32[32,64,64]{2,1,0:T(8,128)}), f32[32,64,64]{2,1,0:T(8,128)}) %all-reduce.11.cloned.1.call-update) | async-done | bytes 524304 | tf_op jit(solution)/shard_map/psum | solution.py:66
  256.0 24.8 %psum.86 = f32[64,64]{0,1:T(8,128)S(1)} all-reduce(f32[64,64]{0,1:T(8,128)S(1)} %convolution_bitcast_fusion.7), channel_id=1, replica_groups=mesh['row'=16,'col'=8] {'col'}, use_global_device_ids=true, to_apply=%region_4.7 | all-reduce | flops 4096 | bytes 32768 | tf_op jit(solution)/shard_map/psum | solution.py:68
  280.9 5.8 cholesky.74
  304.3 13.5 %scatter_fusion.2 = f32[17,64,64]{2,1,0:T(8,128)S(1)} fusion(f32[17,64,64]{2,1,0:T(8,128)S(1)} %broadcast.82.clone.1, s32[128]{0:T(128)S(1)} %get-tuple-element.8, f32[128,64,64]{2,1,0:T(8,128)} %fusion.10), kind=kCustom, calls=%fused_computation.10 | custom fusion | flops 524288 | bytes 6291968 | tf_op jit(solution)/shard_map/scatter-add | solution.py:60
  318.7 57.4 %all-reduce.13.cloned.1.call-done = f32[16,64,64]{2,1,0:T(8,128)} async-done(((f32[16,64,64]{2,1,0:T(8,128)}), f32[16,64,64]{2,1,0:T(8,128)}) %all-reduce.13.cloned.1.call-update) | async-done | bytes 262160 | tf_op jit(solution)/shard_map/psum | solution.py:61
  383.7 13.5 %scatter_fusion.3 = f32[33,64,64]{2,1,0:T(8,128)S(1)} fusion(f32[33,64,64]{2,1,0:T(8,128)S(1)} %broadcast.81.clone.1, s32[128]{0:T(128)S(1)} %get-tuple-element.6, f32[128,64,64]{2,1,0:T(8,128)} %fusion.8), kind=kCustom, calls=%fused_computation.11 | custom fusion | flops 524288 | bytes 6291968 | tf_op jit(solution)/shard_map/scatter-add | solution.py:65
  398.4 86.6 %all-reduce.15.cloned.1.call-done = f32[32,64,64]{2,1,0:T(8,128)} async-done(((f32[32,64,64]{2,1,0:T(8,128)}), f32[32,64,64]{2,1,0:T(8,128)}) %all-reduce.15.cloned.1.call-update) | async-done | bytes 524304 | tf_op jit(solution)/shard_map/psum | solution.py:66
  487.8 24.4 %psum.89 = f32[64,64]{0,1:T(8,128)S(1)} all-reduce(f32[64,64]{0,1:T(8,128)S(1)} %convolution_bitcast_fusion.5), channel_id=1, replica_groups=mesh['row'=16,'col'=8] {'col'}, use_global_device_ids=true, to_apply=%region_11.16 | all-reduce | flops 4096 | bytes 32768 | tf_op jit(solution)/shard_map/psum | solution.py:68
  535.8 13.5 %scatter_fusion.4 = f32[17,64,64]{2,1,0:T(8,128)S(1)} fusion(f32[17,64,64]{2,1,0:T(8,128)S(1)} %broadcast.82.clone, s32[128]{0:T(128)S(1)} %get-tuple-element.8, f32[128,64,64]{2,1,0:T(8,128)} %fusion.6), kind=kCustom, calls=%fused_computation.12 | custom fusion | flops 524288 | bytes 6291968 | tf_op jit(solution)/shard_map/scatter-add | solution.py:60
  550.2 57.4 %all-reduce.17.cloned.1.call-done = f32[16,64,64]{2,1,0:T(8,128)} async-done(((f32[16,64,64]{2,1,0:T(8,128)}), f32[16,64,64]{2,1,0:T(8,128)}) %all-reduce.17.cloned.1.call-update) | async-done | bytes 262160 | tf_op jit(solution)/shard_map/psum | solution.py:61
  615.2 13.5 %scatter_fusion.5 = f32[33,64,64]{2,1,0:T(8,128)S(1)} fusion(f32[33,64,64]{2,1,0:T(8,128)S(1)} %broadcast.81.clone, s32[128]{0:T(128)S(1)} %get-tuple-element.6, f32[128,64,64]{2,1,0:T(8,128)} %fusion.4), kind=kCustom, calls=%fused_computation.13 | custom fusion | flops 524288 | bytes 6291968 | tf_op jit(solution)/shard_map/scatter-add | solution.py:65
  629.9 86.6 %all-reduce.19.cloned.1.call-done = f32[32,64,64]{2,1,0:T(8,128)} async-done(((f32[32,64,64]{2,1,0:T(8,128)}), f32[32,64,64]{2,1,0:T(8,128)}) %all-reduce.19.cloned.1.call-update) | async-done | bytes 524304 | tf_op jit(solution)/shard_map/psum | solution.py:66
  719.3 24.5 %psum.92 = f32[64,64]{0,1:T(8,128)S(1)} all-reduce(f32[64,64]{0,1:T(8,128)S(1)} %convolution_bitcast_fusion.3), channel_id=1, replica_groups=mesh['row'=16,'col'=8] {'col'}, use_global_device_ids=true, to_apply=%region_16.21 | all-reduce | flops 4096 | bytes 32768 | tf_op jit(solution)/shard_map/psum | solution.py:68
  767.3 13.5 %scatter_fusion.6 = f32[17,64,64]{2,1,0:T(8,128)S(1)} fusion(f32[17,64,64]{2,1,0:T(8,128)S(1)} %broadcast.82, s32[128]{0:T(128)S(1)} %get-tuple-element.8, f32[128,64,64]{2,1,0:T(8,128)} %fusion.2), kind=kCustom, calls=%fused_computation.14 | custom fusion | flops 524288 | bytes 6291968 | tf_op jit(solution)/shard_map/scatter-add | solution.py:60
  781.7 57.4 %all-reduce.21.cloned.1.call-done = f32[16,64,64]{2,1,0:T(8,128)} async-done(((f32[16,64,64]{2,1,0:T(8,128)}), f32[16,64,64]{2,1,0:T(8,128)}) %all-reduce.21.cloned.1.call-update) | async-done | bytes 262160 | tf_op jit(solution)/shard_map/psum | solution.py:61
  846.7 13.5 %scatter_fusion.7 = f32[33,64,64]{2,1,0:T(8,128)S(1)} fusion(f32[33,64,64]{2,1,0:T(8,128)S(1)} %broadcast.81, s32[128]{0:T(128)S(1)} %get-tuple-element.6, f32[128,64,64]{2,1,0:T(8,128)} %fusion), kind=kCustom, calls=%fused_computation.15 | custom fusion | flops 524288 | bytes 6291968 | tf_op jit(solution)/shard_map/scatter-add | solution.py:65
  861.4 86.7 %all-reduce.23.cloned.1.call-done = f32[32,64,64]{2,1,0:T(8,128)} async-done(((f32[32,64,64]{2,1,0:T(8,128)}), f32[32,64,64]{2,1,0:T(8,128)}) %all-reduce.23.cloned.1.call-update) | async-done | bytes 524304 | tf_op jit(solution)/shard_map/psum | solution.py:66
  950.8 24.5 %psum.95 = f32[64,64]{0,1:T(8,128)S(1)} all-reduce(f32[64,64]{0,1:T(8,128)S(1)} %convolution_bitcast_fusion.1), channel_id=1, replica_groups=mesh['row'=16,'col'=8] {'col'}, use_global_device_ids=true, to_apply=%region_21.26 | all-reduce | flops 4096 | bytes 32768 | tf_op jit(solution)/shard_map/psum | solution.py:68
  (129 shorter events, 144.4 us)
Async XLA Ops:
  6.5 51.4 %copy-start.4 = (bf16[1,1,128,4096]{3,2,1,0:T(8,128)(2,1)S(1)}, bf16[1,1,128,4096]{3,2,1,0:T(8,128)(2,1)}, u32[]{:S(2)}) copy-start(bf16[1,1,128,4096]{3,2,1,0:T(8,128)(2,1)} %param.14) | copy-start | bytes 3145732
  6.5 137.8 %all-reduce.9.cloned.1.call-start = ((), (), s32[]{:S(2)}) async-start(), calls=%async_computation | async-start | bytes 1048576 | tf_op jit(solution)/shard_map/psum | solution.py:61
  63.6 2.2 copy-start.6
  63.6 2.2 copy-start.7
  70.6 14.5 %copy-start.5 = (f32[2,64]{1,0:T(2,128)S(1)}, f32[2,64]{1,0:T(2,128)}, u32[]{:S(2)}) copy-start(f32[2,64]{1,0:T(2,128)} %param.19) | copy-start | bytes 1540
  85.0 168.2 %all-reduce.11.cloned.1.call-start = ((), (), s32[]{:S(2)}) async-start(), calls=%async_computation.1 | async-start | bytes 2097152 | tf_op jit(solution)/shard_map/psum | solution.py:66
  166.6 209.5 %all-reduce.13.cloned.1.call-start = ((), (), s32[]{:S(2)}) async-start(), calls=%async_computation.2 | async-start | bytes 1048576 | tf_op jit(solution)/shard_map/psum | solution.py:61
  253.2 40.0 %copy-start.1 = (f32[32,64,64]{2,1,0:T(8,128)S(1)}, f32[32,64,64]{2,1,0:T(8,128)}, u32[]{:S(2)}) copy-start(f32[32,64,64]{2,1,0:T(8,128)} %all-reduce.11.cloned.1.call-done) | copy-start | bytes 1572868
  318.7 166.4 %all-reduce.15.cloned.1.call-start = ((), (), s32[]{:S(2)}) async-start(), calls=%async_computation.3 | async-start | bytes 2097152 | tf_op jit(solution)/shard_map/psum | solution.py:66
  398.4 209.2 %all-reduce.17.cloned.1.call-start = ((), (), s32[]{:S(2)}) async-start(), calls=%async_computation.4 | async-start | bytes 1048576 | tf_op jit(solution)/shard_map/psum | solution.py:61
  485.1 39.6 %copy-start.2 = (f32[32,64,64]{2,1,0:T(8,128)S(1)}, f32[32,64,64]{2,1,0:T(8,128)}, u32[]{:S(2)}) copy-start(f32[32,64,64]{2,1,0:T(8,128)} %all-reduce.15.cloned.1.call-done) | copy-start | bytes 1572868
  550.1 166.4 %all-reduce.19.cloned.1.call-start = ((), (), s32[]{:S(2)}) async-start(), calls=%async_computation.5 | async-start | bytes 2097152 | tf_op jit(solution)/shard_map/psum | solution.py:66
  629.9 209.2 %all-reduce.21.cloned.1.call-start = ((), (), s32[]{:S(2)}) async-start(), calls=%async_computation.6 | async-start | bytes 1048576 | tf_op jit(solution)/shard_map/psum | solution.py:61
  716.6 39.7 %copy-start.3 = (f32[32,64,64]{2,1,0:T(8,128)S(1)}, f32[32,64,64]{2,1,0:T(8,128)}, u32[]{:S(2)}) copy-start(f32[32,64,64]{2,1,0:T(8,128)} %all-reduce.19.cloned.1.call-done) | copy-start | bytes 1572868
  781.7 166.4 %all-reduce.23.cloned.1.call-start = ((), (), s32[]{:S(2)}) async-start(), calls=%async_computation.7 | async-start | bytes 2097152 | tf_op jit(solution)/shard_map/psum | solution.py:66
  948.1 39.7 %copy-start = (f32[32,64,64]{2,1,0:T(8,128)S(1)}, f32[32,64,64]{2,1,0:T(8,128)}, u32[]{:S(2)}) copy-start(f32[32,64,64]{2,1,0:T(8,128)} %all-reduce.23.cloned.1.call-done) | copy-start | bytes 1572868
Sparse Core Ops, SparseCore 0:
  85.2 59.1 all-reduce.8
  166.7 86.4 all-reduce.10
  318.8 57.2 all-reduce.12
  398.5 86.4 all-reduce.14
  550.3 57.2 all-reduce.16
  630.0 86.5 all-reduce.18
  781.8 57.2 all-reduce.20
  861.6 86.4 all-reduce.22
where the time goes:
time: 1010 us; the launch traced here: 998 us
  waiting for transfers between devices  567 us (56%)
  other arithmetic  164 us (16%)
  blocking collectives  157 us (16%)
  matrix products  58.3 us (6%)
  local copies, waits for them, and re-layouts  36 us (4%)
  between operations  14.9 us (1%)
    psum x4, waiting for transfers between devices, per_device(): cols_sum = lax.psum(summed[:col_panel], 'row')  346 us
    psum x4, waiting for transfers between devices, per_device(): rows_sum = lax.psum(forward_summed[:row_panel], 'col')  221 us
    psum x4, blocking collectives, per_device(): gram = lax.psum(local_gram(projected), 'col') / total_boxes  98.2 us
    scatter-add x4, other arithmetic, per_device(): summed = jax.ops.segment_sum(product, bwd_ids, num_segments=col_panel + 1)  54.1 us
    scatter-add x4, other arithmetic, per_device(): jax.ops.segment_sum(forward_product, fwd_ids, num_segments=row_panel + 1)  54 us
    another operation x12, other arithmetic, rotate(): lower = jnp.linalg.cholesky(gram)  26.1 us
    all_gather x1, blocking collectives, per_device(): col_mass_panel = lax.all_gather(col_mass, 'row', axis=0, tiled=True)  24.9 us
    all_gather x1, blocking collectives, per_device(): lax.all_gather(vectors, 'row', axis=0, tiled=True)  23.5 us
  transfers between devices with their start and end apart: 8, of which 8 were waited for; matrix products, arithmetic and copies ran while one was open for 0% of the time, Pallas kernels for 0%

commit v1 on v0

--- a/solution.py
+++ b/solution.py
@@ -58,7 +58,7 @@
             "bij,bkj->bki", square, forward_taken, preferred_element_type=jnp.float32
         )
         forward_summed = jax.ops.segment_sum(forward_product, fwd_ids, num_segments=row_panel + 1)
-        rows_sum = lax.psum(forward_summed[:row_panel], "col")
+        rows_sum = jnp.sum(lax.all_gather(forward_summed[:row_panel], "col"), axis=0)
         weighted = (rows_sum * row_mass_panel[:, None, :]).astype(jnp.bfloat16)
         taken = jnp.take(weighted, rows_idx, axis=0)
         product = jnp.einsum("bij,bki->bkj", square, taken, preferred_element_type=jnp.float32)

time: 1010 us -> 904 us (0.90)
  waiting for transfers between devices: 567 us -> 456 us
    psum x4 -> x0, waiting for transfers between devices: 221 us -> none  [per_device(): rows_sum = lax.psum(forward_summed[:row_panel], 'col')]
    all_gather x0 -> x4, waiting for transfers between devices: none -> 106 us  [per_device(): lax.all_gather(forward_summed[:row_panel], 'col')]
    reduce_sum x0 -> x4, other arithmetic: none -> 10.9 us  [per_device(): jnp.sum(lax.all_gather(forward_summed[:row_panel], 'col'), axis=0)]
where the time goes in v1:
time: 904 us; the launch traced here: 893 us
  waiting for transfers between devices  456 us (50%)
  other arithmetic  170 us (19%)
  blocking collectives  157 us (17%)
  matrix products  58.3 us (6%)
  local copies, waits for them, and re-layouts  35.9 us (4%)
  between operations  14.9 us (2%)
    psum x4, waiting for transfers between devices, per_device(): cols_sum = lax.psum(summed[:col_panel], 'row')  349 us
    all_gather x4, waiting for transfers between devices, per_device(): lax.all_gather(forward_summed[:row_panel], 'col')  106 us
    psum x4, blocking collectives, per_device(): gram = lax.psum(local_gram(projected), 'col') / total_boxes  98.2 us
    scatter-add x4, other arithmetic, per_device(): summed = jax.ops.segment_sum(product, bwd_ids, num_segments=col_panel + 1)  54.1 us
    scatter-add x4, other arithmetic, per_device(): jax.ops.segment_sum(forward_product, fwd_ids, num_segments=row_panel + 1)  54 us
    another operation x12, other arithmetic, rotate(): lower = jnp.linalg.cholesky(gram)  26.1 us
    all_gather x1, blocking collectives, per_device(): col_mass_panel = lax.all_gather(col_mass, 'row', axis=0, tiled=True)  24.9 us
    all_gather x1, blocking collectives, per_device(): lax.all_gather(vectors, 'row', axis=0, tiled=True)  23.5 us
  transfers between devices with their start and end apart: 8, of which 8 were waited for; matrix products, arithmetic and copies ran while one was open for 0% of the time, Pallas kernels for 0%

profile of v1, /device:TPU:0, one launch (start us, length us, event | category | flops | bytes accessed | tf_op | source)
XLA Modules:
  0.0 893.0 jit_solution(1445277807393576746)
XLA Ops:
  7.9 24.9 %all-gather.5 = f32[16,2,64]{2,1,0:T(2,128)S(1)} all-gather(f32[1,2,64]{2,1,0:T(2,128)} %bitcast.119), channel_id=1, replica_groups=mesh['row'=16,'col'=8] {'row'}, dimensions={0}, use_global_device_ids=true | all-gather | bytes 8704 | tf_op jit(solution)/shard_map/all_gather | solution.py:50
  32.8 23.5 %all-gather.4 = f32[16,2,4096]{2,1,0:T(2,128)S(1)} all-gather(f32[1,2,4096]{2,1,0:T(2,128)} %bitcast.118), channel_id=1, replica_groups=mesh['row'=16,'col'=8] {'row'}, dimensions={0}, use_global_device_ids=true | all-gather | bytes 557056 | tf_op jit(solution)/shard_map/all_gather | solution.py:53
  70.6 13.5 %scatter_fusion = f32[17,64,64]{2,1,0:T(8,128)S(1)} fusion(f32[17,64,64]{2,1,0:T(8,128)S(1)} %broadcast.82.clone.2, s32[128]{0:T(128)S(1)} %get-tuple-element.8, f32[128,64,64]{2,1,0:T(8,128)} %fusion.14), kind=kCustom, calls=%fused_computation.8 | custom fusion | flops 524288 | bytes 6291968 | tf_op jit(solution)/shard_map/scatter-add | solution.py:60
  85.1 10.7 %all-gather.6 = f32[8,2,64]{2,1,0:T(2,128)S(1)} all-gather(f32[1,2,64]{2,1,0:T(2,128)S(1)} %bitcast.120), channel_id=1, replica_groups=mesh['row'=16,'col'=8] {'col'}, dimensions={0}, use_global_device_ids=true | all-gather | bytes 4608 | tf_op jit(solution)/shard_map/all_gather | solution.py:51
  95.8 20.0 %all-gather.12.cloned.1.call-done = f32[128,64,64]{2,1,0:T(8,128)} async-done(((f32[16,64,64]{2,1,0:T(8,128)}), f32[128,64,64]{2,1,0:T(8,128)}) %all-gather.12.cloned.1.call-update) | async-done | bytes 2097168 | tf_op jit(solution)/shard_map/all_gather | solution.py:61
  125.1 13.5 %scatter_fusion.1 = f32[33,64,64]{2,1,0:T(8,128)S(1)} fusion(f32[33,64,64]{2,1,0:T(8,128)S(1)} %broadcast.81.clone.2, s32[128]{0:T(128)S(1)} %get-tuple-element.6, f32[128,64,64]{2,1,0:T(8,128)} %fusion.12), kind=kCustom, calls=%fused_computation.9 | custom fusion | flops 524288 | bytes 6291968 | tf_op jit(solution)/shard_map/scatter-add | solution.py:65
  139.8 87.4 %all-reduce.5.cloned.1.call-done = f32[32,64,64]{2,1,0:T(8,128)} async-done(((f32[32,64,64]{2,1,0:T(8,128)}), f32[32,64,64]{2,1,0:T(8,128)}) %all-reduce.5.cloned.1.call-update) | async-done | bytes 524304 | tf_op jit(solution)/shard_map/psum | solution.py:66
  229.9 24.8 %psum.57 = f32[64,64]{0,1:T(8,128)S(1)} all-reduce(f32[64,64]{0,1:T(8,128)S(1)} %convolution_bitcast_fusion.7), channel_id=1, replica_groups=mesh['row'=16,'col'=8] {'col'}, use_global_device_ids=true, to_apply=%region_4.7 | all-reduce | flops 4096 | bytes 32768 | tf_op jit(solution)/shard_map/psum | solution.py:68
  254.8 5.8 cholesky.74
  278.2 13.5 %scatter_fusion.2 = f32[17,64,64]{2,1,0:T(8,128)S(1)} fusion(f32[17,64,64]{2,1,0:T(8,128)S(1)} %broadcast.82.clone.1, s32[128]{0:T(128)S(1)} %get-tuple-element.8, f32[128,64,64]{2,1,0:T(8,128)} %fusion.10), kind=kCustom, calls=%fused_computation.10 | custom fusion | flops 524288 | bytes 6291968 | tf_op jit(solution)/shard_map/scatter-add | solution.py:60
  292.6 28.8 %all-gather.14.cloned.1.call-done = f32[128,64,64]{2,1,0:T(8,128)} async-done(((f32[16,64,64]{2,1,0:T(8,128)}), f32[128,64,64]{2,1,0:T(8,128)}) %all-gather.14.cloned.1.call-update) | async-done | bytes 2097168 | tf_op jit(solution)/shard_map/all_gather | solution.py:61
  330.8 13.5 %scatter_fusion.3 = f32[33,64,64]{2,1,0:T(8,128)S(1)} fusion(f32[33,64,64]{2,1,0:T(8,128)S(1)} %broadcast.81.clone.1, s32[128]{0:T(128)S(1)} %get-tuple-element.6, f32[128,64,64]{2,1,0:T(8,128)} %fusion.8), kind=kCustom, calls=%fused_computation.11 | custom fusion | flops 524288 | bytes 6291968 | tf_op jit(solution)/shard_map/scatter-add | solution.py:65
  345.5 87.3 %all-reduce.7.cloned.1.call-done = f32[32,64,64]{2,1,0:T(8,128)} async-done(((f32[32,64,64]{2,1,0:T(8,128)}), f32[32,64,64]{2,1,0:T(8,128)}) %all-reduce.7.cloned.1.call-update) | async-done | bytes 524304 | tf_op jit(solution)/shard_map/psum | solution.py:66
  435.6 24.4 %psum.59 = f32[64,64]{0,1:T(8,128)S(1)} all-reduce(f32[64,64]{0,1:T(8,128)S(1)} %convolution_bitcast_fusion.5), channel_id=1, replica_groups=mesh['row'=16,'col'=8] {'col'}, use_global_device_ids=true, to_apply=%region_11.16 | all-reduce | flops 4096 | bytes 32768 | tf_op jit(solution)/shard_map/psum | solution.py:68
  483.5 13.5 %scatter_fusion.4 = f32[17,64,64]{2,1,0:T(8,128)S(1)} fusion(f32[17,64,64]{2,1,0:T(8,128)S(1)} %broadcast.82.clone, s32[128]{0:T(128)S(1)} %get-tuple-element.8, f32[128,64,64]{2,1,0:T(8,128)} %fusion.6), kind=kCustom, calls=%fused_computation.12 | custom fusion | flops 524288 | bytes 6291968 | tf_op jit(solution)/shard_map/scatter-add | solution.py:60
  497.9 28.8 %all-gather.16.cloned.1.call-done = f32[128,64,64]{2,1,0:T(8,128)} async-done(((f32[16,64,64]{2,1,0:T(8,128)}), f32[128,64,64]{2,1,0:T(8,128)}) %all-gather.16.cloned.1.call-update) | async-done | bytes 2097168 | tf_op jit(solution)/shard_map/all_gather | solution.py:61
  536.1 13.5 %scatter_fusion.5 = f32[33,64,64]{2,1,0:T(8,128)S(1)} fusion(f32[33,64,64]{2,1,0:T(8,128)S(1)} %broadcast.81.clone, s32[128]{0:T(128)S(1)} %get-tuple-element.6, f32[128,64,64]{2,1,0:T(8,128)} %fusion.4), kind=kCustom, calls=%fused_computation.13 | custom fusion | flops 524288 | bytes 6291968 | tf_op jit(solution)/shard_map/scatter-add | solution.py:65
  550.8 87.4 %all-reduce.9.cloned.1.call-done = f32[32,64,64]{2,1,0:T(8,128)} async-done(((f32[32,64,64]{2,1,0:T(8,128)}), f32[32,64,64]{2,1,0:T(8,128)}) %all-reduce.9.cloned.1.call-update) | async-done | bytes 524304 | tf_op jit(solution)/shard_map/psum | solution.py:66
  640.9 24.5 %psum.61 = f32[64,64]{0,1:T(8,128)S(1)} all-reduce(f32[64,64]{0,1:T(8,128)S(1)} %convolution_bitcast_fusion.3), channel_id=1, replica_groups=mesh['row'=16,'col'=8] {'col'}, use_global_device_ids=true, to_apply=%region_16.21 | all-reduce | flops 4096 | bytes 32768 | tf_op jit(solution)/shard_map/psum | solution.py:68
  688.9 13.5 %scatter_fusion.6 = f32[17,64,64]{2,1,0:T(8,128)S(1)} fusion(f32[17,64,64]{2,1,0:T(8,128)S(1)} %broadcast.82, s32[128]{0:T(128)S(1)} %get-tuple-element.8, f32[128,64,64]{2,1,0:T(8,128)} %fusion.2), kind=kCustom, calls=%fused_computation.14 | custom fusion | flops 524288 | bytes 6291968 | tf_op jit(solution)/shard_map/scatter-add | solution.py:60
  703.3 28.8 %all-gather.18.cloned.1.call-done = f32[128,64,64]{2,1,0:T(8,128)} async-done(((f32[16,64,64]{2,1,0:T(8,128)}), f32[128,64,64]{2,1,0:T(8,128)}) %all-gather.18.cloned.1.call-update) | async-done | bytes 2097168 | tf_op jit(solution)/shard_map/all_gather | solution.py:61
  741.5 13.5 %scatter_fusion.7 = f32[33,64,64]{2,1,0:T(8,128)S(1)} fusion(f32[33,64,64]{2,1,0:T(8,128)S(1)} %broadcast.81, s32[128]{0:T(128)S(1)} %get-tuple-element.6, f32[128,64,64]{2,1,0:T(8,128)} %fusion), kind=kCustom, calls=%fused_computation.15 | custom fusion | flops 524288 | bytes 6291968 | tf_op jit(solution)/shard_map/scatter-add | solution.py:65
  756.2 87.4 %all-reduce.11.cloned.1.call-done = f32[32,64,64]{2,1,0:T(8,128)} async-done(((f32[32,64,64]{2,1,0:T(8,128)}), f32[32,64,64]{2,1,0:T(8,128)}) %all-reduce.11.cloned.1.call-update) | async-done | bytes 524304 | tf_op jit(solution)/shard_map/psum | solution.py:66
  846.3 24.5 %psum.63 = f32[64,64]{0,1:T(8,128)S(1)} all-reduce(f32[64,64]{0,1:T(8,128)S(1)} %convolution_bitcast_fusion.1), channel_id=1, replica_groups=mesh['row'=16,'col'=8] {'col'}, use_global_device_ids=true, to_apply=%region_21.26 | all-reduce | flops 4096 | bytes 32768 | tf_op jit(solution)/shard_map/psum | solution.py:68
  (133 shorter events, 151.1 us)
Async XLA Ops:
  6.5 51.4 %copy-start.4 = (bf16[1,1,128,4096]{3,2,1,0:T(8,128)(2,1)S(1)}, bf16[1,1,128,4096]{3,2,1,0:T(8,128)(2,1)}, u32[]{:S(2)}) copy-start(bf16[1,1,128,4096]{3,2,1,0:T(8,128)(2,1)} %param.14) | copy-start | bytes 3145732
  6.5 109.2 %all-gather.12.cloned.1.call-start = ((), (), s32[]{:S(2)}) async-start(), calls=%async_computation.4 | async-start | bytes 4718592 | tf_op jit(solution)/shard_map/all_gather | solution.py:61
  63.6 2.2 copy-start.6
  63.6 2.2 copy-start.7
  70.6 14.4 %copy-start.5 = (f32[2,64]{1,0:T(2,128)S(1)}, f32[2,64]{1,0:T(2,128)}, u32[]{:S(2)}) copy-start(f32[2,64]{1,0:T(2,128)} %param.19) | copy-start | bytes 1540
  85.0 142.1 %all-reduce.5.cloned.1.call-start = ((), (), s32[]{:S(2)}) async-start(), calls=%async_computation | async-start | bytes 2097152 | tf_op jit(solution)/shard_map/psum | solution.py:66
  139.8 181.7 %all-gather.14.cloned.1.call-start = ((), (), s32[]{:S(2)}) async-start(), calls=%async_computation.5 | async-start | bytes 4718592 | tf_op jit(solution)/shard_map/all_gather | solution.py:61
  227.2 40.0 %copy-start.1 = (f32[32,64,64]{2,1,0:T(8,128)S(1)}, f32[32,64,64]{2,1,0:T(8,128)}, u32[]{:S(2)}) copy-start(f32[32,64,64]{2,1,0:T(8,128)} %all-reduce.5.cloned.1.call-done) | copy-start | bytes 1572868
  292.6 140.2 %all-reduce.7.cloned.1.call-start = ((), (), s32[]{:S(2)}) async-start(), calls=%async_computation.1 | async-start | bytes 2097152 | tf_op jit(solution)/shard_map/psum | solution.py:66
  345.4 181.3 %all-gather.16.cloned.1.call-start = ((), (), s32[]{:S(2)}) async-start(), calls=%async_computation.6 | async-start | bytes 4718592 | tf_op jit(solution)/shard_map/all_gather | solution.py:61
  432.8 39.6 %copy-start.2 = (f32[32,64,64]{2,1,0:T(8,128)S(1)}, f32[32,64,64]{2,1,0:T(8,128)}, u32[]{:S(2)}) copy-start(f32[32,64,64]{2,1,0:T(8,128)} %all-reduce.7.cloned.1.call-done) | copy-start | bytes 1572868
  497.9 140.3 %all-reduce.9.cloned.1.call-start = ((), (), s32[]{:S(2)}) async-start(), calls=%async_computation.2 | async-start | bytes 2097152 | tf_op jit(solution)/shard_map/psum | solution.py:66
  550.7 181.4 %all-gather.18.cloned.1.call-start = ((), (), s32[]{:S(2)}) async-start(), calls=%async_computation.7 | async-start | bytes 4718592 | tf_op jit(solution)/shard_map/all_gather | solution.py:61
  638.2 39.7 %copy-start.3 = (f32[32,64,64]{2,1,0:T(8,128)S(1)}, f32[32,64,64]{2,1,0:T(8,128)}, u32[]{:S(2)}) copy-start(f32[32,64,64]{2,1,0:T(8,128)} %all-reduce.9.cloned.1.call-done) | copy-start | bytes 1572868
  703.3 140.3 %all-reduce.11.cloned.1.call-start = ((), (), s32[]{:S(2)}) async-start(), calls=%async_computation.3 | async-start | bytes 2097152 | tf_op jit(solution)/shard_map/psum | solution.py:66
  843.6 39.7 %copy-start = (f32[32,64,64]{2,1,0:T(8,128)S(1)}, f32[32,64,64]{2,1,0:T(8,128)}, u32[]{:S(2)}) copy-start(f32[32,64,64]{2,1,0:T(8,128)} %all-reduce.11.cloned.1.call-done) | copy-start | bytes 1572868
Sparse Core Ops, SparseCore 0:
  85.1 30.5 all-gather.11
  139.9 87.2 all-reduce.4
  292.7 28.6 all-gather.13
  345.6 87.2 all-reduce.6
  498.0 28.6 all-gather.15
  550.9 87.2 all-reduce.8
  703.4 28.6 all-gather.17
  756.3 87.2 all-reduce.10
